TPU v7x, 32 devices: a whole 2x2x4 slice. The times are simulated.
32 devices in a mesh: book: 2 (over y), seq: 4 (over x, core), sub: 4 (over z).
Axes of the slice: x: 2, y: 2, z: 4, core: 2. Of those that a mesh axis runs over, the one named last changes fastest.
Arguments:
- queries: bfloat16 [16384, 2048], P(('book', 'seq'), 'sub'), parts along dimension 0, may hold values from -4 to 1920
- keys: bfloat16 [16384, 2048], P(('book', 'seq'), 'sub'), parts along dimension 0, may hold values from -6 to 4
- values: bfloat16 [16384, 2048], P(('book', 'seq'), 'sub'), parts along dimension 0, may hold values from -6 to 6
- decay: float32 [8, 8], P('book', 'sub'), parts along dimension 0, may hold values from 0.05 to 1
- gate: float32 [8], P('sub'), may hold values from -0.5 to 3
- summary: bfloat16 [512, 2048], P(('book', 'seq')), parts along dimension 0, may hold values from -6 to 6
- wq_sum: bfloat16 [2048, 2048], P(None, 'sub'), may hold values from -0.25 to 0.25
- wo_sum: bfloat16 [2048, 2048], P('sub'), may hold values from -0.125 to 0.125
Outputs:
- attended: bfloat16 [16384, 2048], P(('book', 'seq'), 'sub'), parts along dimension 0
- summarized: bfloat16 [512, 2048], P(('book', 'seq')), parts along dimension 0
There are 2 independent parts, one for each index of `book`. A program takes and returns all parts, laid end to end along the dimension named above; an argument that names none is the same for every part. Nothing has to cross between parts.
All inputs are finite; a program needn't handle non-finite values.
Results may differ from a plain program's by a relative error of at most 0.019.
Values may be sent and summed in bfloat16 or wider, within the bound.
No kernel may reach another device: no remote copies, remote signals or barrier semaphores. Data moves between devices by JAX's collectives and lax.ppermute only.
A program may use at most 128 MiB of HBM per device.

v0:
```python
import jax
import jax.numpy as jnp
from jax import lax
from jax.sharding import PartitionSpec as P

SEG = 2048
STEPS = 4
top_precision = lax.Precision.HIGHEST


def carried_in(value, axis, join, neutral):
    count, mine = (lax.axis_size(axis), lax.axis_index(axis))
    pieces = jax.tree.map(lambda part: lax.all_gather(part, axis), value)
    so_far = jax.tree.map(
        lambda part, zero: jnp.full_like(part, 0) + jnp.asarray(zero, part.dtype), value, neutral
    )

    def step(position, so_far):
        longer = join(so_far, jax.tree.map(lambda part: part[position], pieces))
        return jax.tree.map(lambda new, old: jnp.where(position < mine, new, old), longer, so_far)

    return lax.fori_loop(0, count - 1, step, so_far)


def broadcast(x, axis, root):
    mine = lax.axis_index(axis) == root
    return lax.psum(jnp.where(mine, x, jnp.zeros_like(x)), axis)


def feature_map(inputs):
    return jax.nn.elu(inputs) + 1.0


def head_rms(inputs):
    return inputs * lax.rsqrt(jnp.mean(inputs * inputs, axis=-1, keepdims=True) + 1e-06)


def memory_read(lifted, memory, normalizer):
    numerator = jnp.einsum("qhd,hde->qhe", lifted, memory, precision=top_precision)
    denominator = jnp.einsum("qhd,hd->qh", lifted, normalizer, precision=top_precision) + 1.0
    return numerator / denominator[..., None]


def segment_attention(q_part, k_part, v_part):
    length = q_part.shape[0]
    block_rows = min(512, length)
    score_scale = q_part.shape[2] ** (-0.5)
    columns = jnp.arange(length)
    pieces = []
    for first_row in range(0, length, block_rows):
        scores = (
            jnp.einsum(
                "qhd,khd->hqk",
                q_part[first_row : first_row + block_rows],
                k_part,
                preferred_element_type=jnp.float32,
            )
            * score_scale
        )
        rows_here = first_row + jnp.arange(block_rows)
        scores = jnp.where(columns[None, None, :] <= rows_here[None, :, None], scores, -jnp.inf)
        weights = jax.nn.softmax(scores, axis=-1).astype(jnp.bfloat16)
        pieces.append(
            jnp.einsum("hqk,khd->qhd", weights, v_part, preferred_element_type=jnp.float32)
        )
    return jnp.concatenate(pieces, axis=0)


def on_device(queries, keys, values, decay, gate, summary, wq_sum, wo_sum):
    head_count = gate.shape[0]
    head_width = queries.shape[1] // head_count
    seg_count = queries.shape[0] // SEG
    position = lax.axis_index("seq")
    devices = lax.axis_size("seq")
    q_seg = queries.reshape(seg_count, SEG, head_count, head_width)
    k_seg = keys.reshape(seg_count, SEG, head_count, head_width)
    v_seg = values.reshape(seg_count, SEG, head_count, head_width)
    lifted_keys = feature_map(k_seg.astype(jnp.float32))
    updates = jnp.einsum(
        "jqhd,jqhe->jhde", lifted_keys, v_seg.astype(jnp.float32), precision=top_precision
    )
    key_sums = jnp.sum(lifted_keys, axis=1)
    local_decay = lax.dynamic_slice_in_dim(decay, position * seg_count, seg_count, 0)
    empty_memory = jnp.zeros((head_count, head_width, head_width), jnp.float32)
    empty_norm = jnp.zeros((head_count, head_width), jnp.float32)

    def accumulate(running, inputs_now):
        seg_decay, update, key_total = inputs_now
        return (
            (
                seg_decay[:, None, None] * running[0] + update,
                seg_decay[:, None] * running[1] + key_total,
            ),
            None,
        )

    (own_memory, own_norm), _ = lax.scan(
        accumulate, (empty_memory, empty_norm), (local_decay, updates, key_sums)
    )
    own_decay = jnp.prod(local_decay, axis=0)

    def combine(earlier, later):
        return (
            earlier[0] * later[0],
            later[0][:, None, None] * earlier[1] + later[1],
            later[0][:, None] * earlier[2] + later[2],
        )

    identity = (jnp.ones((head_count,), jnp.float32), empty_memory, empty_norm)
    _, prior_memory, prior_norm = carried_in(
        (own_decay, own_memory, own_norm), "seq", combine, identity
    )
    ending_memory = own_decay[:, None, None] * prior_memory + own_memory
    ending_norm = own_decay[:, None] * prior_norm + own_norm
    final_memory, final_norm = (
        broadcast(ending_memory, "seq", devices - 1),
        broadcast(ending_norm, "seq", devices - 1),
    )
    blend_weight = jax.nn.sigmoid(gate)[None, :, None]

    def one_segment(running, inputs_now):
        memory, normalizer = running
        q_part, k_part, v_part, seg_decay, update, key_total = inputs_now
        recalled = memory_read(feature_map(q_part.astype(jnp.float32)), memory, normalizer)
        local_out = segment_attention(q_part, k_part, v_part)
        mixed = head_rms(blend_weight * recalled + (1.0 - blend_weight) * local_out).astype(
            jnp.bfloat16
        )
        return (
            (
                seg_decay[:, None, None] * memory + update,
                seg_decay[:, None] * normalizer + key_total,
            ),
            mixed,
        )

    _, attended = lax.scan(
        one_segment,
        (prior_memory, prior_norm),
        (q_seg, k_seg, v_seg, local_decay, updates, key_sums),
    )
    attended = attended.reshape(seg_count * SEG, head_count * head_width)
    summary_state = summary
    row_count = summary.shape[0]
    for decode_step in range(STEPS):
        lifted = feature_map(
            jnp.dot(summary_state, wq_sum, preferred_element_type=jnp.float32).reshape(
                row_count, head_count, head_width
            )
        )
        recalled = head_rms(memory_read(lifted, final_memory, final_norm)).astype(jnp.bfloat16)
        partial_out = jnp.dot(
            recalled.reshape(row_count, head_count * head_width),
            wo_sum,
            preferred_element_type=jnp.float32,
        )
        summed = lax.psum(partial_out.astype(jnp.bfloat16), "sub").astype(jnp.float32)
        summary_state = (summary_state.astype(jnp.float32) + summed).astype(jnp.bfloat16)
    return (attended, summary_state)


def solution(mesh):
    placed = (
        P(("book", "seq"), "sub"),
        P(("book", "seq"), "sub"),
        P(("book", "seq"), "sub"),
        P("book", "sub"),
        P("sub"),
        P(("book", "seq"), None),
        P(None, "sub"),
        P("sub", None),
    )
    return jax.shard_map(
        on_device,
        mesh=mesh,
        in_specs=placed,
        out_specs=(P(("book", "seq"), "sub"), P(("book", "seq"), None)),
        check_vma=False,
    )
```

profile of v0, /device:TPU:0, one launch (start us, length us, event | category | flops | bytes accessed | tf_op | source)
XLA Modules:
  0.0 366.3 jit_solution(7190378475324766708)
XLA Ops:
  8.3 7.9 %fusion.73 = f32[2,256,256]{2,1,0:T(8,128)} fusion(bf16[256,2,8,256]{3,2,1,0:T(8,128)(2,1)} %bitcast.224, bf16[256,2,8,256]{3,2,1,0:T(8,128)(2,1)} %bitcast.186, f32[2]{0:T(128)S(1)} %broadcast_multiply_fusion), kind=kOutput, calls=%fused_computation.95 | convolution fusion | flops 3226599424 | bytes 4718600 | tf_op jit(solution)/shard_map/jqhd,jqhe->jhde/dot_general | solution.py:79
  17.9 2.7 fusion.170
  20.6 2.5 convert_element_type.126
  23.1 3.5 fusion.17
  29.3 6.4 %fusion.46 = f32[2,512,2048]{2,1,0:T(8,128)} fusion(bf16[512,2,256]{0,2,1:T(8,128)(2,1)} %bitcast.197, bf16[256,2,8,256]{3,2,1,0:T(8,128)(2,1)} %bitcast.187), kind=kOutput, calls=%fused_computation.76 | convolution fusion | flops 1073741824 | bytes 11010048 | tf_op jit(solution)/shard_map/while/body/eval_jaxpr/qhd,khd->hqk/dot_general | solution.py:52
  39.4 6.4 %fusion.48 = f32[2,512,2048]{2,1,0:T(8,128)} fusion(bf16[512,2,256]{0,2,1:T(8,128)(2,1)} %bitcast.198, bf16[256,2,8,256]{3,2,1,0:T(8,128)(2,1)} %bitcast.188), kind=kOutput, calls=%fused_computation.78 | convolution fusion | flops 1073741824 | bytes 11010048 | tf_op jit(solution)/shard_map/while/body/eval_jaxpr/qhd,khd->hqk/dot_general | solution.py:52
  49.4 6.4 %fusion.50 = f32[2,512,2048]{2,1,0:T(8,128)} fusion(bf16[512,2,256]{0,2,1:T(8,128)(2,1)} %bitcast.199, bf16[256,2,8,256]{3,2,1,0:T(8,128)(2,1)} %bitcast.189), kind=kOutput, calls=%fused_computation.80 | convolution fusion | flops 1073741824 | bytes 11010048 | tf_op jit(solution)/shard_map/while/body/eval_jaxpr/qhd,khd->hqk/dot_general | solution.py:52
  58.4 6.4 %fusion.52 = f32[2,512,2048]{2,1,0:T(8,128)} fusion(bf16[512,2,256]{0,2,1:T(8,128)(2,1)} %bitcast.200, bf16[256,2,8,256]{3,2,1,0:T(8,128)(2,1)} %bitcast.190), kind=kOutput, calls=%fused_computation.82 | convolution fusion | flops 1073741824 | bytes 11010048 | tf_op jit(solution)/shard_map/while/body/eval_jaxpr/qhd,khd->hqk/dot_general | solution.py:52
  65.4 6.1 %all-gather.1 = f32[4,1,2]{2,1,0:T(1,128)} all-gather(f32[1,1,2]{2,1,0:T(1,128)S(1)} %bitcast.214), channel_id=1, replica_groups=mesh['book'=2,'seq'=4,'sub'=4] {'seq'}, dimensions={0}, use_global_device_ids=true | all-gather | bytes 40 | tf_op jit(solution)/shard_map/all_gather | solution.py:13
  71.5 5.6 %all_gather.14 = f32[4,2,256]{2,1,0:T(2,128)S(1)} all-gather(f32[1,2,256]{2,1,0:T(2,128)S(1)} %broadcast_add_fusion), channel_id=1, replica_groups=mesh['book'=2,'seq'=4,'sub'=4] {'seq'}, dimensions={0}, use_global_device_ids=true | all-gather | bytes 10240 | tf_op jit(solution)/shard_map/all_gather | solution.py:13
  77.2 13.3 %fusion.171 = (f32[2,512]{1,0:T(2,128)S(1)}, f32[2,512,2048]{2,1,0:T(8,128)}) fusion(f32[2,512,2048]{2,1,0:T(8,128)} %fusion.46, pred[512,2048]{1,0:T(8,128)(4,1)} %iota_compare_fusion), kind=kOutput, calls=%fused_computation.225 | output fusion | flops 12584959 | bytes 17829888 | tf_op jit(solution)/shard_map/while/body/eval_jaxpr/sub | solution.py:62
  90.4 6.5 %fusion.61 = f32[512,2,256]{0,2,1:T(8,128)} fusion(f32[2,512,2048]{2,1,0:T(8,128)} %get-tuple-element.252, f32[2,512]{1,0:T(2,128)S(1)} %get-tuple-element.251, bf16[256,2,8,256]{3,2,1,0:T(8,128)(2,1)} %bitcast.225), kind=kOutput, calls=%fused_computation.91 | convolution fusion | flops 1077936128 | bytes 11538432 | tf_op jit(solution)/shard_map/while/body/eval_jaxpr/hqk,khd->qhd/dot_general | solution.py:64
  96.9 8.6 %fusion.172 = (f32[2,512]{1,0:T(2,128)S(1)}, f32[2,512,2048]{2,1,0:T(8,128)}) fusion(f32[2,512,2048]{2,1,0:T(8,128)S(1)} %bitcast.193, pred[512,2048]{1,0:T(8,128)(4,1)} %iota_compare_fusion.1), kind=kOutput, calls=%fused_computation.226 | output fusion | flops 12584959 | bytes 17829888 | tf_op jit(solution)/shard_map/while/body/eval_jaxpr/sub | solution.py:62
  105.5 6.5 %fusion.64 = f32[512,2,256]{0,2,1:T(8,128)} fusion(f32[2,512,2048]{2,1,0:T(8,128)} %get-tuple-element.254, f32[2,512]{1,0:T(2,128)S(1)} %get-tuple-element.253, bf16[256,2,8,256]{3,2,1,0:T(8,128)(2,1)} %bitcast.226), kind=kOutput, calls=%fused_computation.92 | convolution fusion | flops 1077936128 | bytes 11538432 | tf_op jit(solution)/shard_map/while/body/eval_jaxpr/hqk,khd->qhd/dot_general | solution.py:64
  112.0 13.2 %fusion.173 = (f32[2,512]{1,0:T(2,128)S(1)}, f32[2,512,2048]{2,1,0:T(8,128)}) fusion(f32[2,512,2048]{2,1,0:T(8,128)} %fusion.50, pred[512,2048]{1,0:T(8,128)(4,1)S(1)} %copy-done.6), kind=kOutput, calls=%fused_computation.227 | output fusion | flops 12584959 | bytes 17829888 | tf_op jit(solution)/shard_map/while/body/eval_jaxpr/sub | solution.py:62
  125.7 12.7 %fusion.174 = (f32[2,512]{1,0:T(2,128)S(1)}, f32[2,512,2048]{2,1,0:T(8,128)}) fusion(f32[2,512,2048]{2,1,0:T(8,128)} %fusion.52, pred[512,2048]{1,0:T(8,128)(4,1)S(1)} %copy-done.5), kind=kOutput, calls=%fused_computation.228 | output fusion | flops 12584959 | bytes 17829888 | tf_op jit(solution)/shard_map/while/body/eval_jaxpr/sub | solution.py:62
  138.4 6.0 %fusion.67 = f32[512,2,256]{0,2,1:T(8,128)} fusion(f32[2,512,2048]{2,1,0:T(8,128)} %get-tuple-element.256, f32[2,512]{1,0:T(2,128)S(1)} %get-tuple-element.255, bf16[256,2,8,256]{3,2,1,0:T(8,128)(2,1)S(1)} %bitcast.227), kind=kOutput, calls=%fused_computation.93 | convolution fusion | flops 1077936128 | bytes 11538432 | tf_op jit(solution)/shard_map/while/body/eval_jaxpr/hqk,khd->qhd/dot_general | solution.py:64
  144.5 2.5 fusion.70
  147.0 5.9 %while.10 = (s32[]{:T(128)}, f32[2,256,256]{2,1,0:T(8,128)S(1)}, f32[2,256]{1,0:T(2,128)S(1)}, s32[]{:T(128)}, f32[4,2]{1,0:T(4,128)}, /*index=5*/f32[4,2,256,25...) while((s32[]{:T(128)}, f32[2,256,256]{2,1,0:T(8,128)S(1)}, f32[2,256]{1,0:T(2,128)S(1)}, ...), condition=%wide.region_2.3_spmd.clone, body=%wide.region_1.2_spmd.clone.sunk | while | flops 526340 | bytes 1579175 | solution.py:22
  153.7 7.3 %psum.43 = f32[2,256]{1,0:T(2,128)S(1)} all-reduce(f32[2,256]{1,0:T(2,128)S(1)} %add_select_fusion.1), channel_id=1, replica_groups=mesh['book'=2,'seq'=4,'sub'=4] {'seq'}, use_global_device_ids=true, to_apply=%region_13.14 | all-reduce | flops 512 | bytes 4096 | tf_op jit(solution)/shard_map/psum | solution.py:27
  162.8 7.0 %fusion.38 = f32[2,1,2048]{2,1,0:T(1,128)S(1)} fusion(f32[256,2,8,256]{3,2,1,0:T(8,128)} %bitcast.194, f32[2,256,1]{1,0,2:T(2,128)S(1)} %bitcast.213), kind=kOutput, calls=%fused_computation.66 | convolution fusion | flops 16777216 | bytes 4212736 | tf_op jit(solution)/shard_map/while/body/eval_jaxpr/qhd,hd->qh/dot_general | solution.py:40
  170.1 26.2 %all-reduce.6.cloned.1.call-done = f32[2,256,256]{2,1,0:T(8,128)} async-done(((f32[2,256,256]{2,1,0:T(8,128)}), f32[2,256,256]{2,1,0:T(8,128)}) %all-reduce.6.cloned.1.call-update) | async-done | bytes 524304 | tf_op jit(solution)/shard_map/psum | solution.py:27
  199.3 35.4 %all-reduce.8.cloned.1.call-done = bf16[64,2048]{1,0:T(8,128)(2,1)} async-done(((bf16[64,2048]{1,0:T(8,128)(2,1)}), bf16[64,2048]{1,0:T(8,128)(2,1)}) %all-reduce.8.cloned.1.call-update) | async-done | bytes 262160 | tf_op jit(solution)/shard_map/psum | solution.py:157
  234.7 2.1 fusion.100
  240.4 17.1 %multiply_reduce_fusion = (f32[2048,2]{0,1:T(2,128)S(1)}, f32[2048,2,256]{0,2,1:T(8,128)}) fusion(f32[512,2,256]{0,2,1:T(8,128)} %fusion.61, f32[512,2,256]{0,2,1:T(8,128)} %fusion.64, f32[512,2,256]{0,2,1:T(8,128)} %fusion.67, f32[512,2,256]{0,2,1:T(8,128)} %fusion.70, f32[2]{0:T(128)S(1)} %copy-done.13, f32[2048,2]{0,1:T(2,128)S(1)} %fusion.134, ...), kind=kOutput, calls=%fused_computation.45 | convolution fusion | flops 3234852864 | bytes 13139984 | tf_op jit(solution)/shard_map/while/body/eval_jaxpr/qhd,hde->qhe/dot_general | solution.py:39
  257.5 17.8 %all-reduce.10.cloned.1.call-done = bf16[64,2048]{1,0:T(8,128)(2,1)} async-done(((bf16[64,2048]{1,0:T(8,128)(2,1)}), bf16[64,2048]{1,0:T(8,128)(2,1)}) %all-reduce.10.cloned.1.call-update) | async-done | bytes 262160 | tf_op jit(solution)/shard_map/psum | solution.py:157
  276.4 2.1 fusion.176
  281.7 35.2 %all-reduce.12.cloned.1.call-done = bf16[64,2048]{1,0:T(8,128)(2,1)} async-done(((bf16[64,2048]{1,0:T(8,128)(2,1)}), bf16[64,2048]{1,0:T(8,128)(2,1)}) %all-reduce.12.cloned.1.call-update) | async-done | bytes 262160 | tf_op jit(solution)/shard_map/psum | solution.py:157
  316.9 2.1 fusion.101
  322.3 4.1 %multiply_convert_fusion = bf16[2048,2,256]{0,2,1:T(8,128)(2,1)} fusion(f32[2048,2,256]{0,2,1:T(8,128)} %get-tuple-element.260, f32[2048,2]{0,1:T(2,128)S(1)} %add_rsqrt_fusion), kind=kLoop, calls=%fused_computation.44 | loop fusion | flops 2097152 | bytes 6307840 | tf_op jit(solution)/shard_map/while/body/eval_jaxpr/convert_element_type | solution.py:126
  326.3 3.9 %copy.135 = bf16[2048,512]{1,0:T(8,128)(2,1)} copy(bf16[2048,512]{0,1:T(8,128)(2,1)} %bitcast.191) | data formatting | bytes 4194304
  330.3 27.2 %all-reduce.14.cloned.1.call-done = bf16[64,2048]{1,0:T(8,128)(2,1)} async-done(((bf16[64,2048]{1,0:T(8,128)(2,1)}), bf16[64,2048]{1,0:T(8,128)(2,1)}) %all-reduce.14.cloned.1.call-update) | async-done | bytes 262160 | tf_op jit(solution)/shard_map/psum | solution.py:157
  (113 shorter events, 41.1 us)
Async XLA Ops:
  7.2 190.9 %copy-start = (bf16[512,2048]{1,0:T(8,128)(2,1)S(1)}, bf16[512,2048]{1,0:T(8,128)(2,1)}, u32[]{:S(2)}) copy-start(bf16[512,2048]{1,0:T(8,128)(2,1)} %param.17) | copy-start | bytes 6291460
  7.2 139.8 %all-gather.4.cloned.1.call-start = ((), (), s32[]{:S(2)}) async-start(), calls=%async_computation.5 | async-start | bytes 2621440 | tf_op jit(solution)/shard_map/all_gather | solution.py:13
  8.2 57.1 %copy-start.9 = (f32[2]{0:T(128)}, f32[2]{0:T(128)S(1)}, u32[]{:S(2)}) copy-start(f32[2]{0:T(128)S(1)} %dynamic-slice_reduce_fusion) | copy-start | bytes 28
  8.2 63.2 %copy-start.10 = (f32[2]{0:T(128)}, f32[2]{0:T(128)S(1)}, u32[]{:S(2)}) copy-start(f32[2]{0:T(128)S(1)} %broadcast_multiply_fusion) | copy-start | bytes 28
  16.2 180.1 %all-reduce.6.cloned.1.call-start = ((), (), s32[]{:S(2)}) async-start(), calls=%async_computation | async-start | bytes 1048576 | tf_op jit(solution)/shard_map/psum | solution.py:27
  16.4 4.2 %copy-start.2 = (bf16[2048,512]{1,0:T(8,128)(2,1)S(1)}, bf16[2048,512]{1,0:T(8,128)(2,1)}, u32[]{:S(2)}) copy-start(bf16[2048,512]{1,0:T(8,128)(2,1)} %param.10) | copy-start | bytes 6291460
  58.4 6.4 %copy-start.12 = (f32[2]{0:T(128)S(1)}, f32[2]{0:T(128)}, u32[]{:S(2)}) copy-start(f32[2]{0:T(128)} %param.14) | copy-start | bytes 28
  77.1 19.8 %slice-start = ((s8[8388608]{0:T(1024)(128)(4,1)}), s8[4194304]{0:T(1024)(128)(4,1)S(1)}, s32[]{:S(2)}) async-start(s8[8388608]{0:T(1024)(128)(4,1)} %bitcast.192), calls=%async_computation.6 | async-start | bytes 8388608
  90.4 6.5 %slice-start.1 = ((s8[8388608]{0:T(1024)(128)(4,1)}), s8[4194304]{0:T(1024)(128)(4,1)S(1)}, s32[]{:S(2)}) async-start(s8[8388608]{0:T(1024)(128)(4,1)} %bitcast.192), calls=%async_computation.7 | async-start | bytes 8388608
  105.5 6.5 %copy-start.6 = (pred[512,2048]{1,0:T(8,128)(4,1)S(1)}, pred[512,2048]{1,0:T(8,128)(4,1)}, u32[]{:S(2)}) copy-start(pred[512,2048]{1,0:T(8,128)(4,1)} %iota_compare_fusion.2) | copy-start | bytes 3145732
  112.0 13.2 %copy-start.1 = (bf16[2048,512]{1,0:T(8,128)(2,1)S(1)}, bf16[2048,512]{1,0:T(8,128)(2,1)}, u32[]{:S(2)}) copy-start(bf16[2048,512]{1,0:T(8,128)(2,1)} %param.16) | copy-start | bytes 6291460
  112.0 13.2 %copy-start.3 = (bf16[64,2048]{1,0:T(8,128)(2,1)S(1)}, bf16[64,2048]{1,0:T(8,128)(2,1)}, u32[]{:S(2)}) copy-start(bf16[64,2048]{1,0:T(8,128)(2,1)} %param.15) | copy-start | bytes 786436
  112.0 13.7 %copy-start.5 = (pred[512,2048]{1,0:T(8,128)(4,1)S(1)}, pred[512,2048]{1,0:T(8,128)(4,1)}, u32[]{:S(2)}) copy-start(pred[512,2048]{1,0:T(8,128)(4,1)} %iota_compare_fusion.3) | copy-start | bytes 3145732
  125.7 12.8 %copy-start.11 = (bf16[2048,512]{1,0:T(8,128)(2,1)S(1)}, bf16[2048,512]{1,0:T(8,128)(2,1)}, u32[]{:S(2)}) copy-start(bf16[2048,512]{1,0:T(8,128)(2,1)} %param.12) | copy-start | bytes 6291460
  138.4 6.0 %copy-start.15 = (f32[2,512,2048]{2,1,0:T(8,128)S(1)}, f32[2,512,2048]{2,1,0:T(8,128)}, u32[]{:S(2)}) copy-start(f32[2,512,2048]{2,1,0:T(8,128)} %get-tuple-element.258) | copy-start | bytes 25165828
  147.0 14.0 %copy-start.4 = (f32[2,256,256]{2,1,0:T(8,128)S(1)}, f32[2,256,256]{2,1,0:T(8,128)}, u32[]{:S(2)}) copy-start(f32[2,256,256]{2,1,0:T(8,128)} %fusion.73) | copy-start | bytes 1572868
  162.6 72.1 %all-reduce.8.cloned.1.call-start = ((), (), s32[]{:S(2)}) async-start(), calls=%async_computation.1 | async-start | bytes 524288 | tf_op jit(solution)/shard_map/psum | solution.py:157
  199.2 41.1 %copy-start.13 = (f32[2]{0:T(128)S(1)}, f32[2]{0:T(128)}, u32[]{:S(2)}) copy-start(f32[2]{0:T(128)} %get-tuple-element.245) | copy-start | bytes 28
  199.2 41.1 %copy-start.14 = (f32[2]{0:T(128)S(1)}, f32[2]{0:T(128)}, u32[]{:S(2)}) copy-start(f32[2]{0:T(128)} %get-tuple-element.246) | copy-start | bytes 28
  199.3 76.0 %all-reduce.10.cloned.1.call-start = ((), (), s32[]{:S(2)}) async-start(), calls=%async_computation.2 | async-start | bytes 524288 | tf_op jit(solution)/shard_map/psum | solution.py:157
  240.1 76.8 %all-reduce.12.cloned.1.call-start = ((), (), s32[]{:S(2)}) async-start(), calls=%async_computation.3 | async-start | bytes 524288 | tf_op jit(solution)/shard_map/psum | solution.py:157
  240.4 34.9 %copy-start.7 = (bf16[64,2048]{1,0:T(8,128)(2,1)S(1)}, bf16[64,2048]{1,0:T(8,128)(2,1)}, u32[]{:S(2)}) copy-start(bf16[64,2048]{1,0:T(8,128)(2,1)} %all-reduce.8.cloned.1.call-done) | copy-start | bytes 786436
  281.7 75.8 %all-reduce.14.cloned.1.call-start = ((), (), s32[]{:S(2)}) async-start(), calls=%async_computation.4 | async-start | bytes 524288 | tf_op jit(solution)/shard_map/psum | solution.py:157
  322.3 35.2 %copy-start.8 = (bf16[64,2048]{1,0:T(8,128)(2,1)S(1)}, bf16[64,2048]{1,0:T(8,128)(2,1)}, u32[]{:S(2)}) copy-start(bf16[64,2048]{1,0:T(8,128)(2,1)} %all-reduce.12.cloned.1.call-done) | copy-start | bytes 786436
Sparse Core Ops, SparseCore 0:
  16.3 25.2 all-gather.3
  162.7 33.5 all-reduce.5
  199.4 35.3 all-reduce.7
  240.2 35.0 all-reduce.9
  281.8 35.0 all-reduce.11
  322.4 35.0 all-reduce.13
where the time goes:
time: 372 us; the launch traced here: 366 us
  waiting for transfers between devices  142 us (38%)
  matrix products  98.1 us (26%)
  other arithmetic  74.2 us (20%)
  blocking collectives  19 us (5%)
  local copies, waits for them, and re-layouts  17.6 us (5%)
  between operations  14.6 us (4%)
    psum x4, waiting for transfers between devices, on_device(): lax.psum(partial_out.astype(jnp.bfloat16), 'sub').astype(jnp.float32)  116 us
    sub x4, other arithmetic, segment_attention(): weights = jax.nn.softmax(scores, axis=-1).astype(jnp.bfloat16)  47.7 us
    psum x1, waiting for transfers between devices, broadcast(): return lax.psum(jnp.where(mine, x, jnp.zeros_like(x)), axis)  26.2 us
    dot_general x4, matrix products, segment_attention(): jnp.einsum('qhd,khd->hqk', q_part[first_row:first_row + block_rows], k_pa...  25.5 us
    dot_general x5, matrix products, memory_read(): jnp.einsum('qhd,hde->qhe', lifted, memory, precision=top_precision)  23.6 us
    dot_general x4, matrix products, segment_attention(): jnp.einsum('hqk,khd->qhd', weights, v_part, preferred_element_type=jnp.fl...  21.6 us
    all_gather x2, blocking collectives, carried_in(): pieces = jax.tree.map(lambda part: lax.all_gather(part, axis), value)  11.7 us
    unnamed x41, local copies, waits for them, and re-layouts  11.2 us
  transfers between devices with their start and end apart: 6, of which 5 were waited for; matrix products, arithmetic and copies ran while one was open for 41% of the time, Pallas kernels for 0%

commit v1 on v0

--- a/solution.py
+++ b/solution.py
@@ -154,7 +154,9 @@
             wo_sum,
             preferred_element_type=jnp.float32,
         )
-        summed = lax.psum(partial_out.astype(jnp.bfloat16), "sub").astype(jnp.float32)
+        summed = jnp.sum(lax.all_gather(partial_out.astype(jnp.bfloat16), "sub"), axis=0).astype(
+            jnp.float32
+        )
         summary_state = (summary_state.astype(jnp.float32) + summed).astype(jnp.bfloat16)
     return (attended, summary_state)
 

time: 372 us -> 305 us (0.82)
  waiting for transfers between devices: 142 us -> 74.4 us
    psum x4 -> x0, waiting for transfers between devices: 116 us -> none  [on_device(): lax.psum(partial_out.astype(jnp.bfloat16), 'sub').astype(jnp.float32)]
    all_gather x0 -> x4, waiting for transfers between devices: none -> 41 us  [on_device(): lax.all_gather(partial_out.astype(jnp.bfloat16), 'sub')]
    psum x1, waiting for transfers between devices: 26.2 us -> 33.3 us  [broadcast(): return lax.psum(jnp.where(mine, x, jnp.zeros_like(x)), axis)]
    reduce_sum x0 -> x4, other arithmetic: none -> 6.37 us  [on_device(): jnp.sum(lax.all_gather(partial_out.astype(jnp.bfloat16), 'sub'), axis=0)]
    unnamed x41 -> x27, local copies, waits for them, and re-layouts: 11.2 us -> 13.1 us
  transfers between devices with their start and end apart: 6 -> 6, of which waited for: 5 -> 5; matrix products, arithmetic and copies ran while one was open for 41% -> 49% of each run, Pallas kernels for 0% -> 0%
where the time goes in v1:
time: 305 us; the launch traced here: 300 us
  matrix products  98.4 us (32%)
  other arithmetic  75.5 us (25%)
  waiting for transfers between devices  74.4 us (24%)
  blocking collectives  19 us (6%)
  local copies, waits for them, and re-layouts  16.9 us (6%)
  between operations  14.7 us (5%)
    sub x4, other arithmetic, segment_attention(): weights = jax.nn.softmax(scores, axis=-1).astype(jnp.bfloat16)  48.6 us
    all_gather x4, waiting for transfers between devices, on_device(): lax.all_gather(partial_out.astype(jnp.bfloat16), 'sub')  41 us
    psum x1, waiting for transfers between devices, broadcast(): return lax.psum(jnp.where(mine, x, jnp.zeros_like(x)), axis)  33.3 us
    dot_general x4, matrix products, segment_attention(): jnp.einsum('qhd,khd->hqk', q_part[first_row:first_row + block_rows], k_pa...  25.8 us
    dot_general x4, matrix products, segment_attention(): jnp.einsum('hqk,khd->qhd', weights, v_part, preferred_element_type=jnp.fl...  25 us
    dot_general x5, matrix products, memory_read(): jnp.einsum('qhd,hde->qhe', lifted, memory, precision=top_precision)  22.6 us
    unnamed x27, local copies, waits for them, and re-layouts  13.1 us
    all_gather x2, blocking collectives, carried_in(): pieces = jax.tree.map(lambda part: lax.all_gather(part, axis), value)  11.8 us
  transfers between devices with their start and end apart: 6, of which 5 were waited for; matrix products, arithmetic and copies ran while one was open for 49% of the time, Pallas kernels for 0%

profile of v1, /device:TPU:0, one launch (start us, length us, event | category | flops | bytes accessed | tf_op | source)
XLA Modules:
  0.0 300.0 jit_solution(10122963186352952920)
XLA Ops:
  8.2 7.9 %fusion.73 = f32[2,256,256]{2,1,0:T(8,128)} fusion(bf16[256,2,8,256]{3,2,1,0:T(8,128)(2,1)} %bitcast.232, bf16[256,2,8,256]{3,2,1,0:T(8,128)(2,1)} %bitcast.190, f32[2]{0:T(128)S(1)} %broadcast_multiply_fusion), kind=kOutput, calls=%fused_computation.95 | convolution fusion | flops 3226599424 | bytes 4718600 | tf_op jit(solution)/shard_map/jqhd,jqhe->jhde/dot_general | solution.py:79
  16.4 3.5 %fusion.17 = f32[512]{0:T(512)S(1)} fusion(bf16[2048,512]{1,0:T(8,128)(2,1)} %param.11), kind=kLoop, calls=%fused_computation.37 | loop fusion | flops 6290944 | bytes 2099200 | tf_op jit(solution)/shard_map/reduce_sum | solution.py:82
  19.9 2.7 fusion.170
  22.6 2.1 copy.157
  24.7 6.6 %fusion.46 = f32[2,512,2048]{2,1,0:T(8,128)} fusion(bf16[512,2,256]{0,2,1:T(8,128)(2,1)} %bitcast.202, bf16[256,2,8,256]{3,2,1,0:T(8,128)(2,1)} %bitcast.191), kind=kOutput, calls=%fused_computation.76 | convolution fusion | flops 1073741824 | bytes 11010048 | tf_op jit(solution)/shard_map/while/body/eval_jaxpr/qhd,khd->hqk/dot_general | solution.py:52
  32.9 2.1 copy.156
  34.9 6.4 %fusion.48 = f32[2,512,2048]{2,1,0:T(8,128)} fusion(bf16[512,2,256]{0,2,1:T(8,128)(2,1)} %bitcast.203, bf16[256,2,8,256]{3,2,1,0:T(8,128)(2,1)} %bitcast.192), kind=kOutput, calls=%fused_computation.78 | convolution fusion | flops 1073741824 | bytes 11010048 | tf_op jit(solution)/shard_map/while/body/eval_jaxpr/qhd,khd->hqk/dot_general | solution.py:52
  45.0 6.4 %fusion.50 = f32[2,512,2048]{2,1,0:T(8,128)} fusion(bf16[512,2,256]{0,2,1:T(8,128)(2,1)} %bitcast.204, bf16[256,2,8,256]{3,2,1,0:T(8,128)(2,1)} %bitcast.193), kind=kOutput, calls=%fused_computation.80 | convolution fusion | flops 1073741824 | bytes 11010048 | tf_op jit(solution)/shard_map/while/body/eval_jaxpr/qhd,khd->hqk/dot_general | solution.py:52
  54.0 6.1 %all-gather.5 = f32[4,1,2]{2,1,0:T(1,128)S(1)} all-gather(f32[1,1,2]{2,1,0:T(1,128)S(1)} %bitcast.222), channel_id=1, replica_groups=mesh['book'=2,'seq'=4,'sub'=4] {'seq'}, dimensions={0}, use_global_device_ids=true | all-gather | bytes 40 | tf_op jit(solution)/shard_map/all_gather | solution.py:13
  60.2 5.6 %all_gather.38 = f32[4,2,256]{2,1,0:T(2,128)S(1)} all-gather(f32[1,2,256]{2,1,0:T(2,128)S(1)} %broadcast_add_fusion), channel_id=1, replica_groups=mesh['book'=2,'seq'=4,'sub'=4] {'seq'}, dimensions={0}, use_global_device_ids=true | all-gather | bytes 10240 | tf_op jit(solution)/shard_map/all_gather | solution.py:13
  65.8 13.3 %fusion.171 = (f32[2,512]{1,0:T(2,128)S(1)}, f32[2,512,2048]{2,1,0:T(8,128)}) fusion(f32[2,512,2048]{2,1,0:T(8,128)} %fusion.46, pred[512,2048]{1,0:T(8,128)(4,1)} %iota_compare_fusion), kind=kOutput, calls=%fused_computation.225 | output fusion | flops 12584959 | bytes 17829888 | tf_op jit(solution)/shard_map/while/body/eval_jaxpr/sub | solution.py:62
  79.6 13.4 %fusion.172 = (f32[2,512]{1,0:T(2,128)S(1)}, f32[2,512,2048]{2,1,0:T(8,128)}) fusion(f32[2,512,2048]{2,1,0:T(8,128)} %fusion.48, pred[512,2048]{1,0:T(8,128)(4,1)} %iota_compare_fusion.1), kind=kOutput, calls=%fused_computation.226 | output fusion | flops 12584959 | bytes 17829888 | tf_op jit(solution)/shard_map/while/body/eval_jaxpr/sub | solution.py:62
  93.0 8.5 %fusion.173 = (f32[2,512]{1,0:T(2,128)S(1)}, f32[2,512,2048]{2,1,0:T(8,128)}) fusion(f32[2,512,2048]{2,1,0:T(8,128)S(1)} %bitcast.197, pred[512,2048]{1,0:T(8,128)(4,1)} %iota_compare_fusion.2), kind=kOutput, calls=%fused_computation.227 | output fusion | flops 12584959 | bytes 17829888 | tf_op jit(solution)/shard_map/while/body/eval_jaxpr/sub | solution.py:62
  101.5 6.6 %fusion.61 = f32[512,2,256]{0,2,1:T(8,128)} fusion(f32[2,512,2048]{2,1,0:T(8,128)} %get-tuple-element.252, f32[2,512]{1,0:T(2,128)S(1)} %get-tuple-element.251, bf16[256,2,8,256]{3,2,1,0:T(8,128)(2,1)} %bitcast.233), kind=kOutput, calls=%fused_computation.91 | convolution fusion | flops 1077936128 | bytes 11538432 | tf_op jit(solution)/shard_map/while/body/eval_jaxpr/hqk,khd->qhd/dot_general | solution.py:64
  108.1 3.8 %while.10 = (s32[]{:T(128)}, f32[2,256,256]{2,1,0:T(8,128)S(1)}, f32[2,256]{1,0:T(2,128)S(1)}, s32[]{:T(128)}, f32[4,2]{1,0:T(4,128)S(1)}, /*index=5*/f32[4,2,25...) while((s32[]{:T(128)}, f32[2,256,256]{2,1,0:T(8,128)S(1)}, ...), condition=%wide.region_2.3_spmd.clone, body=%wide.region_1.2_spmd.clone.sunk | while | flops 526340 | bytes 1579175 | solution.py:22
  112.0 7.3 %psum.15 = f32[2,256]{1,0:T(2,128)S(1)} all-reduce(f32[2,256]{1,0:T(2,128)S(1)} %add_select_fusion.1), channel_id=1, replica_groups=mesh['book'=2,'seq'=4,'sub'=4] {'seq'}, use_global_device_ids=true, to_apply=%region_13.14 | all-reduce | flops 512 | bytes 4096 | tf_op jit(solution)/shard_map/psum | solution.py:27
  121.5 33.3 %all-reduce.2.cloned.1.call-done = f32[2,256,256]{2,1,0:T(8,128)} async-done(((f32[2,256,256]{2,1,0:T(8,128)}), f32[2,256,256]{2,1,0:T(8,128)}) %all-reduce.2.cloned.1.call-update) | async-done | bytes 524304 | tf_op jit(solution)/shard_map/psum | solution.py:27
  157.9 6.5 %fusion.52 = f32[2,512,2048]{2,1,0:T(8,128)} fusion(bf16[512,2,256]{0,2,1:T(8,128)(2,1)} %bitcast.201, bf16[256,2,8,256]{3,2,1,0:T(8,128)(2,1)} %bitcast.194), kind=kOutput, calls=%fused_computation.82 | convolution fusion | flops 1073741824 | bytes 11010048 | tf_op jit(solution)/shard_map/while/body/eval_jaxpr/qhd,khd->hqk/dot_general | solution.py:52
  165.9 6.0 %fusion.64 = f32[512,2,256]{0,2,1:T(8,128)} fusion(f32[2,512,2048]{2,1,0:T(8,128)} %get-tuple-element.254, f32[2,512]{1,0:T(2,128)S(1)} %get-tuple-element.253, bf16[256,2,8,256]{3,2,1,0:T(8,128)(2,1)S(1)} %bitcast.235), kind=kOutput, calls=%fused_computation.92 | convolution fusion | flops 1077936128 | bytes 11538432 | tf_op jit(solution)/shard_map/while/body/eval_jaxpr/hqk,khd->qhd/dot_general | solution.py:64
  171.8 14.1 %all-gather.14.cloned.1.call-done = bf16[256,2048]{1,0:T(8,128)(2,1)} async-done(((bf16[64,2048]{1,0:T(8,128)(2,1)}), bf16[256,2048]{1,0:T(8,128)(2,1)}) %all-gather.14.cloned.1.call-update) | async-done | bytes 1048592 | tf_op jit(solution)/shard_map/all_gather | solution.py:157
  187.3 2.1 fusion.100
  193.2 13.4 %fusion.174 = (f32[2,512]{1,0:T(2,128)S(1)}, f32[2,512,2048]{2,1,0:T(8,128)}) fusion(f32[2,512,2048]{2,1,0:T(8,128)} %fusion.52, pred[512,2048]{1,0:T(8,128)(4,1)} %iota_compare_fusion.3), kind=kOutput, calls=%fused_computation.228 | output fusion | flops 12584959 | bytes 17829888 | tf_op jit(solution)/shard_map/while/body/eval_jaxpr/sub | solution.py:62
  206.6 5.9 %fusion.67 = f32[512,2,256]{0,2,1:T(8,128)} fusion(f32[2,512,2048]{2,1,0:T(8,128)} %get-tuple-element.256, f32[2,512]{1,0:T(2,128)S(1)} %get-tuple-element.255, bf16[256,2,8,256]{3,2,1,0:T(8,128)(2,1)S(1)} %bitcast.236), kind=kOutput, calls=%fused_computation.93 | convolution fusion | flops 1077936128 | bytes 11538432 | tf_op jit(solution)/shard_map/while/body/eval_jaxpr/hqk,khd->qhd/dot_general | solution.py:64
  212.6 7.7 %all-gather.16.cloned.1.call-done = bf16[256,2048]{1,0:T(8,128)(2,1)} async-done(((bf16[64,2048]{1,0:T(8,128)(2,1)}), bf16[256,2048]{1,0:T(8,128)(2,1)}) %all-gather.16.cloned.1.call-update) | async-done | bytes 1048592 | tf_op jit(solution)/shard_map/all_gather | solution.py:157
  220.3 2.2 reduce_sum.155
  223.6 2.1 fusion.176
  229.1 6.5 %fusion.70 = f32[512,2,256]{0,2,1:T(8,128)} fusion(f32[2,512,2048]{2,1,0:T(8,128)} %get-tuple-element.258, f32[2,512]{1,0:T(2,128)S(1)} %get-tuple-element.257, bf16[256,2,8,256]{3,2,1,0:T(8,128)(2,1)} %bitcast.234), kind=kOutput, calls=%fused_computation.94 | convolution fusion | flops 1077936128 | bytes 11538432 | tf_op jit(solution)/shard_map/while/body/eval_jaxpr/hqk,khd->qhd/dot_general | solution.py:64
  238.2 4.8 %fusion.38 = f32[2,1,2048]{2,1,0:T(1,128)S(1)} fusion(f32[256,2,8,256]{3,2,1,0:T(8,128)S(1)} %bitcast.198, f32[2,256,1]{1,0,2:T(2,128)S(1)} %bitcast.221), kind=kOutput, calls=%fused_computation.66 | convolution fusion | flops 16777216 | bytes 4212736 | tf_op jit(solution)/shard_map/while/body/eval_jaxpr/qhd,hd->qh/dot_general | solution.py:40
  243.0 13.5 %all-gather.18.cloned.1.call-done = bf16[256,2048]{1,0:T(8,128)(2,1)} async-done(((bf16[64,2048]{1,0:T(8,128)(2,1)}), bf16[256,2048]{1,0:T(8,128)(2,1)}) %all-gather.18.cloned.1.call-update) | async-done | bytes 1048592 | tf_op jit(solution)/shard_map/all_gather | solution.py:157
  263.1 16.1 %multiply_reduce_fusion = (f32[2048,2]{0,1:T(2,128)S(1)}, f32[2048,2,256]{0,2,1:T(8,128)S(1)}) fusion(f32[512,2,256]{0,2,1:T(8,128)} %fusion.61, f32[512,2,256]{0,2,1:T(8,128)} %fusion.64, f32[512,2,256]{0,2,1:T(8,128)} %fusion.67, f32[512,2,256]{0,2,1:T(8,128)} %fusion.70, f32[2]{0:T(128)S(1)} %get-tuple-element.245, f32[2048,2]{0,1:T(2,128)S(1)} %fusion.134, ...), kind=kOutput, calls=%fused_computation.45 | convolution fusion | flops 3234852864 | bytes 13139984 | tf_op jit(solution)/shard_map/while/body/eval_jaxpr/qhd,hde->qhe/dot_general | solution.py:39
  281.1 3.9 %copy.135 = bf16[2048,512]{1,0:T(8,128)(2,1)} copy(bf16[2048,512]{0,1:T(8,128)(2,1)} %bitcast.195) | data formatting | bytes 4194304
  285.0 5.7 %all-gather.20.cloned.1.call-done = bf16[256,2048]{1,0:T(8,128)(2,1)} async-done(((bf16[64,2048]{1,0:T(8,128)(2,1)}), bf16[256,2048]{1,0:T(8,128)(2,1)}) %all-gather.20.cloned.1.call-update) | async-done | bytes 1048592 | tf_op jit(solution)/shard_map/all_gather | solution.py:157
  (103 shorter events, 43.4 us)
Async XLA Ops:
  7.2 149.4 %copy-start = (bf16[512,2048]{1,0:T(8,128)(2,1)S(1)}, bf16[512,2048]{1,0:T(8,128)(2,1)}, u32[]{:S(2)}) copy-start(bf16[512,2048]{1,0:T(8,128)(2,1)} %param.17) | copy-start | bytes 6291460
  7.2 100.9 %all-gather.12.cloned.1.call-start = ((), (), s32[]{:S(2)}) async-start(), calls=%async_computation.1 | async-start | bytes 2621440 | tf_op jit(solution)/shard_map/all_gather | solution.py:13
  16.1 138.7 %all-reduce.2.cloned.1.call-start = ((), (), s32[]{:S(2)}) async-start(), calls=%async_computation | async-start | bytes 1048576 | tf_op jit(solution)/shard_map/psum | solution.py:27
  65.8 13.3 %copy-start.1 = (bf16[2048,512]{1,0:T(8,128)(2,1)S(1)}, bf16[2048,512]{1,0:T(8,128)(2,1)}, u32[]{:S(2)}) copy-start(bf16[2048,512]{1,0:T(8,128)(2,1)} %param.16) | copy-start | bytes 6291460
  65.8 13.3 %copy-start.4 = (bf16[64,2048]{1,0:T(8,128)(2,1)S(1)}, bf16[64,2048]{1,0:T(8,128)(2,1)}, u32[]{:S(2)}) copy-start(bf16[64,2048]{1,0:T(8,128)(2,1)} %param.15) | copy-start | bytes 786436
  79.1 13.9 %slice-start = ((s8[8388608]{0:T(1024)(128)(4,1)}), s8[4194304]{0:T(1024)(128)(4,1)S(1)}, s32[]{:S(2)}) async-start(s8[8388608]{0:T(1024)(128)(4,1)} %bitcast.196), calls=%async_computation.6 | async-start | bytes 8388608
  79.6 13.4 %slice-start.1 = ((s8[8388608]{0:T(1024)(128)(4,1)}), s8[4194304]{0:T(1024)(128)(4,1)S(1)}, s32[]{:S(2)}) async-start(s8[8388608]{0:T(1024)(128)(4,1)} %bitcast.196), calls=%async_computation.7 | async-start | bytes 8388608
  121.2 64.7 %all-gather.14.cloned.1.call-start = ((), (), s32[]{:S(2)}) async-start(), calls=%async_computation.2 | async-start | bytes 1310720 | tf_op jit(solution)/shard_map/all_gather | solution.py:157
  157.8 62.5 %all-gather.16.cloned.1.call-start = ((), (), s32[]{:S(2)}) async-start(), calls=%async_computation.3 | async-start | bytes 1310720 | tf_op jit(solution)/shard_map/all_gather | solution.py:157
  157.9 8.0 %copy-start.6 = (bf16[2048,512]{1,0:T(8,128)(2,1)S(1)}, bf16[2048,512]{1,0:T(8,128)(2,1)}, u32[]{:S(2)}) copy-start(bf16[2048,512]{1,0:T(8,128)(2,1)} %param.12) | copy-start | bytes 6291460
  187.3 19.3 %copy-start.5 = (bf16[64,2048]{1,0:T(8,128)(2,1)}, bf16[64,2048]{1,0:T(8,128)(2,1)S(1)}, u32[]{:S(2)}) copy-start(bf16[64,2048]{1,0:T(8,128)(2,1)S(1)} %reduce_sum.153) | copy-start | bytes 786436
  192.7 63.8 %all-gather.18.cloned.1.call-start = ((), (), s32[]{:S(2)}) async-start(), calls=%async_computation.4 | async-start | bytes 1310720 | tf_op jit(solution)/shard_map/all_gather | solution.py:157
  193.2 13.4 %copy-start.7 = (bf16[2048,512]{1,0:T(8,128)(2,1)S(1)}, bf16[2048,512]{1,0:T(8,128)(2,1)}, u32[]{:S(2)}) copy-start(bf16[2048,512]{1,0:T(8,128)(2,1)} %param.12) | copy-start | bytes 6291460
  228.9 61.8 %all-gather.20.cloned.1.call-start = ((), (), s32[]{:S(2)}) async-start(), calls=%async_computation.5 | async-start | bytes 1310720 | tf_op jit(solution)/shard_map/all_gather | solution.py:157
  229.1 6.5 %copy-start.2 = (bf16[2048,512]{1,0:T(8,128)(2,1)S(1)}, bf16[2048,512]{1,0:T(8,128)(2,1)}, u32[]{:S(2)}) copy-start(bf16[2048,512]{1,0:T(8,128)(2,1)} %param.10) | copy-start | bytes 6291460
  235.6 0.7 copy-start.8
  236.3 1.9 copy-start.3
Sparse Core Ops, SparseCore 0:
  16.3 25.2 all-gather.11
  121.3 33.4 all-reduce.1
  157.9 27.9 all-gather.13
  192.8 27.4 all-gather.15
  229.0 27.4 all-gather.17
  263.2 27.4 all-gather.19
